TPU v7x, 128 devices: a whole 4x4x4 slice. The times are simulated.
128 devices in a mesh: row: 16 (over y, x), col: 8 (over z, core).
Axes of the slice: x: 4, y: 4, z: 4, core: 2. Of those that a mesh axis runs over, the one named last changes fastest.
Arguments:
- snapshots: float32 [65536, 2048], P(('row', 'col')), may hold values from -6 to 6
- district: int32 [65536], P(('row', 'col')), may hold values from 0 to 255, never falling along the last dimension, each value on 1 to 1024 neighbouring positions
- target: int32 [65536], replicated, may hold values from 0 to 65535, as said below
Outputs:
- coefficients: float32 [512, 2048], P(None, 'col')
- remainder: float32 [65536, 2048], P('row', 'col')
Inputs may be any that keep to these rules, and one draw needn't show every extreme that they name: A permutation of the storage rows; each aligned block of 512 nodes has exactly 512 / 16 nodes whose target lies in each aligned block of 4096 storage rows. `district`: districts never fall along the nodes, and each holds at most 1024 nodes.
All inputs are finite; a program needn't handle non-finite values.
Results may differ from a plain program's by a relative error of at most 0.0001.
Values sent between devices are 32-bit elements; how exact they have to be, the bound alone decides.
A program may use at most 128 MiB of HBM per device.

v0:
```python
import jax
import jax.numpy as jnp
from jax import lax
from jax.sharding import PartitionSpec as P

NB = 256
DIST_MEAN = 256
HIGH = lax.Precision.HIGHEST


def from_root(value, axis, source):
    kept = jnp.where(lax.axis_index(axis) == source, value, 0).astype(value.dtype)
    return lax.psum(kept, axis)


def orthonormal(panel, gram):
    lower = jnp.linalg.cholesky(gram)
    inverse = jax.scipy.linalg.solve_triangular(
        lower, jnp.eye(gram.shape[0], dtype=gram.dtype), lower=True
    )
    return jnp.dot(panel, inverse.T, precision=HIGH)


def gram_of(panel):
    return jnp.dot(panel.T, panel, precision=HIGH)


def body(snapshots, district, target):
    n_row = lax.axis_size("row")
    n_col = lax.axis_size("col")
    nodes_dev, snaps = snapshots.shape
    nodes = target.shape[0]
    groups = nodes // DIST_MEAN
    labels = jnp.arange(groups, dtype=jnp.int32)
    member = (district[:, None] == labels[None, :]).astype(jnp.float32)
    counts = lax.psum(jnp.sum(member, axis=0), ("row", "col"))
    scale = jnp.sqrt(DIST_MEAN / jnp.maximum(counts, 1.0))
    weight = jnp.dot(member, scale, precision=HIGH)
    weighted = snapshots * weight[:, None]
    local_rows = nodes // n_row
    per_owner = nodes_dev // n_row
    width = snaps // n_col
    source = lax.axis_index(("row", "col"))
    mine = lax.dynamic_slice_in_dim(target, source * nodes_dev, nodes_dev)
    owner = mine // local_rows
    order = jnp.argsort(owner * nodes_dev + jnp.arange(nodes_dev, dtype=jnp.int32))
    sorted_rows = weighted[order]
    shaped = sorted_rows.reshape(n_row, per_owner, width // NB, n_col, NB)
    shaped = shaped.transpose(0, 3, 1, 2, 4).reshape(n_row, n_col, per_owner, width)
    moved = lax.all_to_all(
        shaped.reshape(n_row * n_col, per_owner, width),
        ("row", "col"),
        split_axis=0,
        concat_axis=0,
        tiled=True,
    )
    arrived = moved.reshape(n_row * n_col * per_owner, width)
    my_row = lax.axis_index("row")
    chosen = jnp.nonzero(target // local_rows == my_row, size=local_rows)[0]
    placing = target[chosen] % local_rows
    inverse = (
        jnp.zeros((local_rows,), jnp.int32).at[placing].set(jnp.arange(local_rows, dtype=jnp.int32))
    )
    block = arrived[inverse]
    stacked = []
    for index in range(2):
        first = index // n_col * NB
        panel = block
        gram = lax.psum(gram_of(panel), "row")
        basis = from_root(orthonormal(panel, gram), "col", index % n_col)
        projection = lax.psum(jnp.dot(basis.T, block, precision=HIGH), "row")
        block = block - jnp.dot(basis, projection, precision=HIGH)
        stacked.append(projection)
    return (jnp.concatenate(stacked, axis=0), block)


def solution(mesh):
    in_specs = (P(("row", "col"), None), P(("row", "col")), P())
    out_specs = (P(None, "col"), P("row", "col"))
    return jax.shard_map(body, mesh=mesh, in_specs=in_specs, out_specs=out_specs, check_vma=False)
```

profile of v0, /device:TPU:0, one launch (start us, length us, event | category | flops | bytes accessed | tf_op | source)
XLA Modules:
  0.0 1310.8 jit_solution(6391460466063920243)
XLA Ops:
  12.6 68.2 %psum.49 = f32[256]{0:T(256)S(1)} all-reduce(f32[256]{0:T(256)S(1)} %convert_reduce_fusion), channel_id=1, replica_groups=mesh['row'=16,'col'=8] {'row','col'}, use_global_device_ids=true, to_apply=%region_1.0 | all-reduce | flops 256 | bytes 2048 | tf_op jit(solution)/shard_map/psum | solution.py:36
  109.9 452.2 %scatter_custom_fusion = s32[4096]{0:T(1024)S(1)} fusion(s32[65536]{0:T(1024)S(1)} %bitcast.103, s32[65536]{0:T(1024)S(1)} %ne.84, s32[]{:T(128)} %copy.53), kind=kCustom, calls=%fused_computation.94 | custom fusion | flops 65536 | bytes 16388 | tf_op jit(solution)/shard_map/scatter-add | solution.py:59
  563.4 23.0 %gather_fusion.1 = s32[4096]{0:T(1024)S(1)} fusion(s32[65536]{0:T(1024)S(1)} %copy-done, s32[4096]{0:T(1024)S(1)} %broadcast_clamp_fusion), kind=kCustom, calls=%fused_computation.1 | custom fusion | bytes 49152 | tf_op jit(solution)/shard_map/gather | solution.py:60
  586.6 15.5 %scatter_custom_fusion.1 = s32[4096]{0:T(1024)S(1)} fusion(s32[4096]{0:T(1024)S(1)} %bitcast.108, s32[4096]{0:T(1024)S(1)} %iota.77, s32[]{:T(128)} %copy.53), kind=kCustom, calls=%fused_computation.92 | custom fusion | bytes 16388 | tf_op jit(solution)/shard_map/scatter | solution.py:62
  602.1 18.3 %gather_fusion.2 = f32[4096,256]{1,0:T(8,128)} fusion(f32[4096,256]{1,0:T(8,128)} %bitcast.4, s32[4096]{0:T(1024)S(1)} %fusion.28), kind=kCustom, calls=%fused_computation.2 | custom fusion | bytes 8404992 | tf_op jit(solution)/shard_map/gather | solution.py:64
  620.4 10.9 fusion.44
  631.7 84.8 %all-reduce.9.cloned.1.call-done = f32[256,256]{0,1:T(8,128)} async-done(((f32[256,256]{0,1:T(8,128)}), f32[256,256]{0,1:T(8,128)}) %all-reduce.9.cloned.1.call-update) | async-done | bytes 262160 | tf_op jit(solution)/shard_map/psum | solution.py:69
  718.6 11.7 cholesky.130
  730.4 9.8 custom-call.13
  740.7 11.7 cholesky.147
  759.1 19.7 %custom-call.14 = f32[2,128,128]{1,2,0:T(8,128)S(1)} custom-call(f32[2,128,128]{2,1,0:T(8,128)S(1)} %get-tuple-element.20), custom_call_target="InvertDiagBlocksLowerTriangular" | custom-call | tf_op jit(solution)/shard_map/jit(_solve_triangular)/triangular_solve | solution.py:18
  779.7 7.6 convolution_select_fusion.1
  787.4 72.5 %all-reduce.11.cloned.1.call-done = f32[4096,256]{1,0:T(8,128)} async-done(((f32[4096,256]{1,0:T(8,128)}), f32[4096,256]{1,0:T(8,128)}) %all-reduce.11.cloned.1.call-update) | async-done | bytes 4194320 | tf_op jit(solution)/shard_map/psum | solution.py:13
  859.9 10.9 fusion.45
  871.1 83.8 %all-reduce.13.cloned.1.call-done = f32[256,256]{1,0:T(8,128)} async-done(((f32[256,256]{1,0:T(8,128)}), f32[256,256]{1,0:T(8,128)}) %all-reduce.13.cloned.1.call-update) | async-done | bytes 262160 | tf_op jit(solution)/shard_map/psum | solution.py:71
  971.6 83.3 %all-reduce.15.cloned.1.call-done = f32[256,256]{0,1:T(8,128)} async-done(((f32[256,256]{0,1:T(8,128)}), f32[256,256]{0,1:T(8,128)}) %all-reduce.15.cloned.1.call-update) | async-done | bytes 262160 | tf_op jit(solution)/shard_map/psum | solution.py:69
  1057.0 11.7 cholesky.164
  1068.8 9.8 custom-call.15
  1079.1 11.7 cholesky.181
  1098.1 19.7 %custom-call.16 = f32[2,128,128]{1,2,0:T(8,128)S(1)} custom-call(f32[2,128,128]{2,1,0:T(8,128)S(1)} %get-tuple-element.21), custom_call_target="InvertDiagBlocksLowerTriangular" | custom-call | tf_op jit(solution)/shard_map/jit(_solve_triangular)/triangular_solve | solution.py:18
  1126.6 72.4 %all-reduce.17.cloned.1.call-done = f32[4096,256]{1,0:T(8,128)} async-done(((f32[4096,256]{1,0:T(8,128)}), f32[4096,256]{1,0:T(8,128)}) %all-reduce.17.cloned.1.call-update) | async-done | bytes 4194320 | tf_op jit(solution)/shard_map/psum | solution.py:13
  1198.9 10.9 fusion.47
  1209.9 84.0 %all-reduce.19.cloned.1.call-done = f32[256,256]{1,0:T(8,128)} async-done(((f32[256,256]{1,0:T(8,128)}), f32[256,256]{1,0:T(8,128)}) %all-reduce.19.cloned.1.call-update) | async-done | bytes 262160 | tf_op jit(solution)/shard_map/psum | solution.py:71
  1293.9 9.0 convolution_subtract_fusion
  (109 shorter events, 88.2 us)
Async XLA Ops:
  101.4 6.0 copy-start
  101.4 500.7 %all-to-all-start = ((f32[128,32,256]{2,1,0:T(8,128)}), f32[128,32,256]{2,1,0:T(8,128)}, u32[]{:S(2)}, u32[]{:S(2)}) async-start(f32[128,32,256]{2,1,0:T(8,128)} %bitcast.100), calls=%async_computation | async-start | bytes 8388608 | tf_op jit(solution)/shard_map/all_to_all | solution.py:50
  107.4 609.1 %all-reduce.9.cloned.1.call-start = ((), (), s32[]{:S(2)}) async-start(), calls=%async_computation.1 | async-start | bytes 524288 | tf_op jit(solution)/shard_map/psum | solution.py:69
  631.4 228.6 %all-reduce.11.cloned.1.call-start = ((), (), s32[]{:S(2)}) async-start(), calls=%async_computation.2 | async-start | bytes 8388608 | tf_op jit(solution)/shard_map/psum | solution.py:13
  787.4 167.6 %all-reduce.13.cloned.1.call-start = ((), (), s32[]{:S(2)}) async-start(), calls=%async_computation.3 | async-start | bytes 524288 | tf_op jit(solution)/shard_map/psum | solution.py:71
  870.9 184.1 %all-reduce.15.cloned.1.call-start = ((), (), s32[]{:S(2)}) async-start(), calls=%async_computation.4 | async-start | bytes 524288 | tf_op jit(solution)/shard_map/psum | solution.py:69
  961.9 2.0 copy-start.1
  971.4 227.5 %all-reduce.17.cloned.1.call-start = ((), (), s32[]{:S(2)}) async-start(), calls=%async_computation.5 | async-start | bytes 8388608 | tf_op jit(solution)/shard_map/psum | solution.py:13
  1126.4 167.6 %all-reduce.19.cloned.1.call-start = ((), (), s32[]{:S(2)}) async-start(), calls=%async_computation.6 | async-start | bytes 524288 | tf_op jit(solution)/shard_map/psum | solution.py:71
  1209.9 93.1 %copy-start.2 = (f32[256,256]{1,0:T(8,128)S(1)}, f32[256,256]{1,0:T(8,128)}, u32[]{:S(2)}) copy-start(f32[256,256]{1,0:T(8,128)} %all-reduce.13.cloned.1.call-done) | copy-start | bytes 786436
  1293.9 9.0 copy-start.3
Sparse Core Ops, SparseCore 0:
  631.5 84.9 all-reduce.8
  787.5 72.4 all-reduce.10
  871.0 83.8 all-reduce.12
  971.5 83.3 all-reduce.14
  1126.5 72.4 all-reduce.16
  1210.0 83.8 all-reduce.18
where the time goes:
time: 1320 us; the launch traced here: 1310 us
  other arithmetic  576 us (44%)
  waiting for transfers between devices  481 us (36%)
  local copies, waits for them, and re-layouts  85.1 us (6%)
  matrix products  75.2 us (6%)
  blocking collectives  68.2 us (5%)
  between operations  17.4 us (1%)
    scatter-add x1, other arithmetic, body(): chosen = jnp.nonzero(target // local_rows == my_row, size=local_rows)[0]  452 us
    psum x2, waiting for transfers between devices, body(): gram = lax.psum(gram_of(panel), 'row')  168 us
    psum x2, waiting for transfers between devices, body(): projection = lax.psum(jnp.dot(basis.T, block, precision=HIGH), 'row')  168 us
    psum x2, waiting for transfers between devices, from_root(): return lax.psum(kept, axis)  145 us
    another operation x13, other arithmetic, orthonormal(): lower = jnp.linalg.cholesky(gram)  68.7 us
    psum x1, blocking collectives, body(): counts = lax.psum(jnp.sum(member, axis=0), ('row', 'col'))  68.2 us
    another operation x5, other arithmetic, orthonormal(): jax.scipy.linalg.solve_triangular(lower, jnp.eye(gram.shape[0], dtype=gra...  39.4 us
  transfers between devices with their start and end apart: 7, of which 6 were waited for; matrix products, arithmetic and copies ran while one was open for 38% of the time, Pallas kernels for 0%

commit v1 on v0

--- a/solution.py
+++ b/solution.py
@@ -1,3 +1,4 @@
+import functools
 import jax
 import jax.numpy as jnp
 from jax import lax
@@ -6,6 +7,13 @@
 NB = 256
 DIST_MEAN = 256
 HIGH = lax.Precision.HIGHEST
+
+
+def apply_face(my_data, chip_axis):
+    return jnp.sum(lax.all_gather(my_data, axis_name=chip_axis), 0)
+
+
+point_the_edge = functools.partial(apply_face, chip_axis="row")
 
 
 def from_root(value, axis, source):
@@ -68,7 +76,7 @@
         panel = block
         gram = lax.psum(gram_of(panel), "row")
         basis = from_root(orthonormal(panel, gram), "col", index % n_col)
-        projection = lax.psum(jnp.dot(basis.T, block, precision=HIGH), "row")
+        projection = point_the_edge(jnp.dot(basis.T, block, precision=HIGH))
         block = block - jnp.dot(basis, projection, precision=HIGH)
         stacked.append(projection)
     return (jnp.concatenate(stacked, axis=0), block)

time: 1320 us -> 1260 us (0.955)
  waiting for transfers between devices: 481 us -> 416 us
    psum x2 -> x0, waiting for transfers between devices: 168 us -> none  [body(): projection = lax.psum(jnp.dot(basis.T, block, precision=HIGH), 'row')]
    all_gather x0 -> x2, waiting for transfers between devices: none -> 103 us  [apply_face(): return jnp.sum(lax.all_gather(my_data, axis_name=chip_axis), 0)]
  transfers between devices with their start and end apart: 7 -> 7, of which waited for: 6 -> 6; matrix products, arithmetic and copies ran while one was open for 38% -> 40% of each run, Pallas kernels for 0% -> 0%
where the time goes in v1:
time: 1260 us; the launch traced here: 1250 us
  other arithmetic  581 us (46%)
  waiting for transfers between devices  416 us (33%)
  local copies, waits for them, and re-layouts  85.1 us (7%)
  matrix products  74.9 us (6%)
  blocking collectives  68.2 us (5%)
  between operations  17.4 us (1%)
    scatter-add x1, other arithmetic, body(): chosen = jnp.nonzero(target // local_rows == my_row, size=local_rows)[0]  452 us
    psum x2, waiting for transfers between devices, body(): gram = lax.psum(gram_of(panel), 'row')  168 us
    psum x2, waiting for transfers between devices, from_root(): return lax.psum(kept, axis)  145 us
    all_gather x2, waiting for transfers between devices, apply_face(): return jnp.sum(lax.all_gather(my_data, axis_name=chip_axis), 0)  103 us
    another operation x13, other arithmetic, orthonormal(): lower = jnp.linalg.cholesky(gram)  68.7 us
    psum x1, blocking collectives, body(): counts = lax.psum(jnp.sum(member, axis=0), ('row', 'col'))  68.2 us
    another operation x5, other arithmetic, orthonormal(): jax.scipy.linalg.solve_triangular(lower, jnp.eye(gram.shape[0], dtype=gra...  39.4 us
  transfers between devices with their start and end apart: 7, of which 6 were waited for; matrix products, arithmetic and copies ran while one was open for 40% of the time, Pallas kernels for 0%

profile of v1, /device:TPU:0, one launch (start us, length us, event | category | flops | bytes accessed | tf_op | source)
XLA Modules:
  0.0 1250.6 jit_solution(17631276507633062015)
XLA Ops:
  12.6 68.2 %psum.35 = f32[256]{0:T(256)S(1)} all-reduce(f32[256]{0:T(256)S(1)} %convert_reduce_fusion), channel_id=1, replica_groups=mesh['row'=16,'col'=8] {'row','col'}, use_global_device_ids=true, to_apply=%region_1.0 | all-reduce | flops 256 | bytes 2048 | tf_op jit(solution)/shard_map/psum | solution.py:44
  109.9 452.2 %scatter_custom_fusion = s32[4096]{0:T(1024)S(1)} fusion(s32[65536]{0:T(1024)S(1)} %bitcast.107, s32[65536]{0:T(1024)S(1)} %ne.84, s32[]{:T(128)} %copy.53), kind=kCustom, calls=%fused_computation.94 | custom fusion | flops 65536 | bytes 16388 | tf_op jit(solution)/shard_map/scatter-add | solution.py:67
  563.4 23.0 %gather_fusion.1 = s32[4096]{0:T(1024)S(1)} fusion(s32[65536]{0:T(1024)S(1)} %copy-done, s32[4096]{0:T(1024)S(1)} %broadcast_clamp_fusion), kind=kCustom, calls=%fused_computation.1 | custom fusion | bytes 49152 | tf_op jit(solution)/shard_map/gather | solution.py:68
  586.6 15.5 %scatter_custom_fusion.1 = s32[4096]{0:T(1024)S(1)} fusion(s32[4096]{0:T(1024)S(1)} %bitcast.112, s32[4096]{0:T(1024)S(1)} %iota.77, s32[]{:T(128)} %copy.53), kind=kCustom, calls=%fused_computation.92 | custom fusion | bytes 16388 | tf_op jit(solution)/shard_map/scatter | solution.py:70
  602.1 18.3 %gather_fusion.2 = f32[4096,256]{1,0:T(8,128)} fusion(f32[4096,256]{1,0:T(8,128)} %bitcast.4, s32[4096]{0:T(1024)S(1)} %fusion.28), kind=kCustom, calls=%fused_computation.2 | custom fusion | bytes 8404992 | tf_op jit(solution)/shard_map/gather | solution.py:72
  620.4 10.9 fusion.44
  631.7 84.8 %all-reduce.7.cloned.1.call-done = f32[256,256]{0,1:T(8,128)} async-done(((f32[256,256]{0,1:T(8,128)}), f32[256,256]{0,1:T(8,128)}) %all-reduce.7.cloned.1.call-update) | async-done | bytes 262160 | tf_op jit(solution)/shard_map/psum | solution.py:77
  718.6 11.7 cholesky.130
  730.4 9.8 custom-call.13
  740.7 11.7 cholesky.147
  759.1 19.7 %custom-call.14 = f32[2,128,128]{1,2,0:T(8,128)S(1)} custom-call(f32[2,128,128]{2,1,0:T(8,128)S(1)} %get-tuple-element.20), custom_call_target="InvertDiagBlocksLowerTriangular" | custom-call | tf_op jit(solution)/shard_map/jit(_solve_triangular)/triangular_solve | solution.py:26
  779.7 7.6 convolution_select_fusion.1
  787.4 72.5 %all-reduce.9.cloned.1.call-done = f32[4096,256]{1,0:T(8,128)} async-done(((f32[4096,256]{1,0:T(8,128)}), f32[4096,256]{1,0:T(8,128)}) %all-reduce.9.cloned.1.call-update) | async-done | bytes 4194320 | tf_op jit(solution)/shard_map/psum | solution.py:21
  859.9 10.9 fusion.45
  871.1 51.2 %all-gather.5.cloned.1.call-done = f32[4096,256]{1,0:T(8,128)} async-done(((f32[256,256]{1,0:T(8,128)}), f32[4096,256]{1,0:T(8,128)}) %all-gather.5.cloned.1.call-update) | async-done | bytes 4194320 | tf_op jit(solution)/shard_map/all_gather | solution.py:13
  941.4 83.6 %all-reduce.11.cloned.1.call-done = f32[256,256]{0,1:T(8,128)} async-done(((f32[256,256]{0,1:T(8,128)}), f32[256,256]{0,1:T(8,128)}) %all-reduce.11.cloned.1.call-update) | async-done | bytes 262160 | tf_op jit(solution)/shard_map/psum | solution.py:77
  1027.1 11.7 cholesky.164
  1038.9 9.8 custom-call.15
  1049.2 11.7 cholesky.181
  1068.2 19.7 %custom-call.16 = f32[2,128,128]{1,2,0:T(8,128)S(1)} custom-call(f32[2,128,128]{2,1,0:T(8,128)S(1)} %get-tuple-element.21), custom_call_target="InvertDiagBlocksLowerTriangular" | custom-call | tf_op jit(solution)/shard_map/jit(_solve_triangular)/triangular_solve | solution.py:26
  1096.6 72.3 %all-reduce.13.cloned.1.call-done = f32[4096,256]{1,0:T(8,128)} async-done(((f32[4096,256]{1,0:T(8,128)}), f32[4096,256]{1,0:T(8,128)}) %all-reduce.13.cloned.1.call-update) | async-done | bytes 4194320 | tf_op jit(solution)/shard_map/psum | solution.py:21
  1169.0 10.9 fusion.47
  1179.9 51.4 %all-gather.7.cloned.1.call-done = f32[4096,256]{1,0:T(8,128)} async-done(((f32[256,256]{1,0:T(8,128)}), f32[4096,256]{1,0:T(8,128)}) %all-gather.7.cloned.1.call-update) | async-done | bytes 4194320 | tf_op jit(solution)/shard_map/all_gather | solution.py:13
  1234.7 8.9 convolution_subtract_fusion
  (107 shorter events, 93.1 us)
Async XLA Ops:
  101.4 6.0 copy-start
  101.4 500.7 %all-to-all-start = ((f32[128,32,256]{2,1,0:T(8,128)}), f32[128,32,256]{2,1,0:T(8,128)}, u32[]{:S(2)}, u32[]{:S(2)}) async-start(f32[128,32,256]{2,1,0:T(8,128)} %bitcast.102), calls=%async_computation | async-start | bytes 8388608 | tf_op jit(solution)/shard_map/all_to_all | solution.py:58
  107.4 609.1 %all-reduce.7.cloned.1.call-start = ((), (), s32[]{:S(2)}) async-start(), calls=%async_computation.1 | async-start | bytes 524288 | tf_op jit(solution)/shard_map/psum | solution.py:77
  631.4 228.5 %all-reduce.9.cloned.1.call-start = ((), (), s32[]{:S(2)}) async-start(), calls=%async_computation.2 | async-start | bytes 8388608 | tf_op jit(solution)/shard_map/psum | solution.py:21
  787.3 135.0 %all-gather.5.cloned.1.call-start = ((), (), s32[]{:S(2)}) async-start(), calls=%async_computation.5 | async-start | bytes 4456448 | tf_op jit(solution)/shard_map/all_gather | solution.py:13
  870.8 154.2 %all-reduce.11.cloned.1.call-start = ((), (), s32[]{:S(2)}) async-start(), calls=%async_computation.3 | async-start | bytes 524288 | tf_op jit(solution)/shard_map/psum | solution.py:77
  931.7 2.0 copy-start.1
  941.1 227.8 %all-reduce.13.cloned.1.call-start = ((), (), s32[]{:S(2)}) async-start(), calls=%async_computation.4 | async-start | bytes 8388608 | tf_op jit(solution)/shard_map/psum | solution.py:21
  1096.4 134.9 %all-gather.7.cloned.1.call-start = ((), (), s32[]{:S(2)}) async-start(), calls=%async_computation.6 | async-start | bytes 4456448 | tf_op jit(solution)/shard_map/all_gather | solution.py:13
Sparse Core Ops, SparseCore 0:
  631.5 84.9 all-reduce.6
  787.5 72.3 all-reduce.8
  871.0 51.2 all-gather.4
  941.3 83.6 all-reduce.10
  1096.5 72.3 all-reduce.12
  1180.0 51.2 all-gather.6
